TPU v7x, 256 devices: a whole 4x4x8 slice. The times are simulated.
256 devices in a mesh: dp: 4 (over x), seq: 8 (over z), tensor: 8 (over y, core).
Axes of the slice: x: 4, y: 4, z: 8, core: 2. Of those that a mesh axis runs over, the one named last changes fastest.
Arguments:
- query_vectors: bfloat16 [1792, 4096], P(('dp', 'seq'), 'tensor'), may hold values from -128 to 128
- key_vectors: bfloat16 [1792, 2048], P(('dp', 'seq'), 'tensor'), may hold values from -6 to 6
- value_vectors: bfloat16 [1792, 2048], P(('dp', 'seq'), 'tensor'), may hold values from -6 to 6
- out_weight: bfloat16 [4096, 3584], P(None, 'tensor'), may hold values from -0.09375 to 0.09375
- residual: bfloat16 [1792, 3584], P(('dp', 'seq'), 'tensor'), may hold values from -64 to 64
- post_gain: float32 [3584], P('tensor'), may hold values from 0.1 to 1.9
- final_gain: float32 [3584], P('tensor'), may hold values from 0.1 to 1.9
- vocab_weight: bfloat16 [128000, 3584], P(('dp', 'seq', 'tensor')), may hold values from -4 to 4
- segment_ids: int32 [4, 448], P('dp', 'seq'), may hold values from 0 to 7, as said below
- doc_starts: int32 [4, 8], P('dp'), may hold values from 0 to 447, as said below
- doc_index: int32 [4, 8], P('dp'), may hold values from 0 to 31
- targets: int32 [4, 448], replicated, may hold values from 0 to 127999
Outputs:
- token_logprob: float32 [4, 448], P('dp', 'seq')
- doc_loglik: float32 [32], replicated
- doc_counts: float32 [32], replicated
Inputs may be any that keep to these rules, and one draw needn't show every extreme that they name: `segment_ids`: within each row the numbers never fall and every number 0 to 7 appears; segment s of a row begins at doc_starts[row, s]; each segment holds 1 to 336 positions. doc_starts[row, 0] = 0 and the starts rise strictly along each row.
All inputs are finite; a program needn't handle non-finite values.
Results may differ from a plain program's by a relative error of at most 0.00074.
Values may be sent and summed in bfloat16 or wider, within the bound.
No kernel may reach another device: no remote copies, remote signals or barrier semaphores. Data moves between devices by JAX's collectives and lax.ppermute only.
A program may use at most 64 MiB of HBM per device.

v0:
```python
import jax
import jax.numpy as jnp
from jax import lax
from jax.sharding import Mesh
from jax.sharding import PartitionSpec as P

D = 3584
HEAD_DIM = 256
TENSOR = ("tensor_0", "tensor_1")
DP_SEQ_TENSOR = ("dp", "seq", "tensor_0", "tensor_1")


ATTENTION_CAP = 50.0
LOGIT_CAP = 30.0
EPSILON = 1e-06


def side_by_side(arrays, axis, dim, along):
    ends, at = ([], 0)
    for a in arrays[:-1]:
        at += a.shape[along]
        ends.append(at)
    both = jnp.concatenate(arrays, axis=along)
    return tuple(jnp.split(lax.all_gather(both, axis, axis=dim, tiled=True), ends, axis=along))


def laid_out(blocks, dim):
    blocks = jnp.moveaxis(blocks, 0, dim)
    lengths = blocks.shape
    return blocks.reshape(*lengths[:dim], lengths[dim] * lengths[dim + 1], *lengths[dim + 2 :])


def copy_for_each(shard, axis):
    size = lax.axis_size(axis)
    return lax.all_to_all(
        jnp.broadcast_to(shard[None], (size, *shard.shape)), axis, 0, 0, tiled=True
    )


def collect(shard, axis, dim):
    return laid_out(copy_for_each(shard, axis), dim)


def over_copies(shard, axis):
    return copy_for_each(shard, axis).sum(axis=0)


def together(arrays, axis):
    ends = [0]
    for a in arrays:
        ends.append(ends[-1] + a.size)
    total = over_copies(jnp.concatenate([a.ravel() for a in arrays]), axis)
    return tuple((total[b:e].reshape(a.shape) for a, b, e in zip(arrays, ends, ends[1:])))


def cut_along(shard, dim, size):
    before, after = (shard.shape[:dim], shard.shape[dim + 1 :])
    return jnp.moveaxis(shard.reshape(*before, size, -1, *after), dim, 0)


def summed_on_arrival(shard, axis, dim):
    size = lax.axis_size(axis)
    blocks = lax.all_to_all(cut_along(shard, dim, size), axis, 0, 0, tiled=True)
    return jnp.sum(blocks, axis=0)


def summed_rows(shard, axes, dim):
    far, near = axes
    blocks = cut_along(shard, dim, lax.axis_size(far))
    nearer = summed_on_arrival(blocks, near, dim + 1)
    arrived = lax.all_to_all(nearer, far, split_axis=0, concat_axis=0, tiled=True)
    return arrived.sum(axis=0)


def over_axes(shard, axes):
    far, near = axes
    nearer = over_copies(shard, near)
    return over_copies(nearer, far)


def in_one(arrays, axis):
    flat, at, finished = (jnp.concatenate([a.reshape(-1) for a in arrays]), 0, [])
    total = over_axes(flat, axis)
    for a in arrays:
        finished.append(total[at : at + a.size].reshape(a.shape))
        at += a.size
    return tuple(finished)


def local(
    query_vectors,
    key_vectors,
    value_vectors,
    out_weight,
    residual,
    post_gain,
    final_gain,
    vocab_weight,
    segment_ids,
    doc_starts,
    doc_index,
    targets,
):
    tok_rows = query_vectors.shape[0]
    seg_row = segment_ids[0]
    starts = doc_starts[0]
    seg_count = starts.shape[0]
    slot_ids = jnp.arange(seg_count, dtype=jnp.int32)
    positions = lax.axis_index("seq") * tok_rows + jnp.arange(tok_rows, dtype=jnp.int32)
    doc_first = jnp.sum(
        jnp.where(seg_row[:, None] == slot_ids[None, :], starts[None, :], 0), axis=1
    )
    local_groups = key_vectors.shape[1] // HEAD_DIM
    group_size = query_vectors.shape[1] // key_vectors.shape[1]
    query_heads = query_vectors.reshape(tok_rows, local_groups, group_size, HEAD_DIM)
    score_scale = HEAD_DIM ** (-0.5)
    key_block, value_block = side_by_side((key_vectors, value_vectors), "seq", 0, 1)
    row_count = key_block.shape[0]
    key_heads = key_block.reshape(row_count, local_groups, HEAD_DIM)
    value_heads = value_block.reshape(row_count, local_groups, HEAD_DIM)
    raw_scores = jnp.einsum(
        "ikgd,jkd->ikgj", query_heads, key_heads, preferred_element_type=jnp.float32
    )
    capped = ATTENTION_CAP * jnp.tanh(raw_scores * score_scale / ATTENTION_CAP)
    key_positions = jnp.arange(row_count, dtype=jnp.int32)
    visible = (key_positions[None, :] <= positions[:, None]) & (
        key_positions[None, :] >= doc_first[:, None]
    )
    weights = jnp.where(visible[:, None, None, :], jnp.exp(capped), 0.0)
    rounded = weights.astype(jnp.bfloat16)
    numerator = jnp.einsum(
        "ikgj,jkd->ikgd", rounded, value_heads, preferred_element_type=jnp.float32
    )
    denominator = jnp.sum(weights, axis=-1)
    numerator, denominator = (numerator, denominator)
    attended = (
        (numerator / denominator[..., None])
        .reshape(tok_rows, query_vectors.shape[1])
        .astype(jnp.bfloat16)
    )
    branch = jnp.dot(collect(attended, TENSOR, 1), out_weight, preferred_element_type=jnp.float32)
    carried_in = residual.astype(jnp.float32)
    gained = post_gain[None, :] * branch
    sq_branch, sq_carried, cross_sum, sq_gained = together(
        (
            jnp.sum(branch * branch, axis=1),
            jnp.sum(carried_in * carried_in, axis=1),
            jnp.sum(carried_in * gained, axis=1),
            jnp.sum(gained * gained, axis=1),
        ),
        TENSOR,
    )
    inv_branch = 1.0 / jnp.sqrt(sq_branch / D + EPSILON)
    updated = carried_in + gained * inv_branch[:, None]
    sq_total = sq_carried + 2.0 * inv_branch * cross_sum + inv_branch * inv_branch * sq_gained
    hidden = (final_gain[None, :] * updated / jnp.sqrt(sq_total / D + EPSILON)[:, None]).astype(
        jnp.bfloat16
    )
    vocab_count = vocab_weight.shape[0]
    tensor_size = lax.axis_size(TENSOR)
    seq_size = lax.axis_size("seq")
    labels = targets.reshape(-1)
    flat_index = (
        lax.axis_index("dp") * seq_size + lax.axis_index("seq")
    ) * tensor_size + lax.axis_index(TENSOR)
    vocab_ids = flat_index * vocab_count + jnp.arange(vocab_count, dtype=jnp.int32)
    features = collect(hidden, TENSOR, 1)
    block_in = lax.all_gather(features, ("dp", "seq"), axis=0, tiled=True)
    logits = lax.dot_general(
        vocab_weight, block_in, (((1,), (1,)), ((), ())), preferred_element_type=jnp.float32
    )
    capped = LOGIT_CAP * jnp.tanh(logits / LOGIT_CAP)
    totals = jnp.sum(jnp.exp(capped), axis=0)
    chosen = jnp.sum(jnp.where(vocab_ids[:, None] == labels[None, :], capped, 0.0), axis=0)
    partial_value = jnp.stack([totals, chosen])
    totals, chosen = (
        summed_rows(partial_value[0], (("dp", "seq"), ("tensor_0", "tensor_1")), 0),
        summed_rows(partial_value[1], (("dp", "seq"), ("tensor_0", "tensor_1")), 0),
    )
    share_len = totals.shape[0]
    offset_rows = lax.axis_index(TENSOR) * share_len
    seg_share = lax.dynamic_slice_in_dim(seg_row, offset_rows, share_len)
    pos_share = lax.dynamic_slice_in_dim(positions, offset_rows, share_len)
    next_segment = seg_share + 1
    doc_end = jnp.sum(
        jnp.where(slot_ids[None, :] == next_segment[:, None], starts[None, :], 0), axis=1
    )
    doc_end = doc_end + jnp.where(next_segment == seg_count, tok_rows * seq_size, 0)
    counted = (pos_share + 1 < doc_end).astype(jnp.float32)
    logprob = counted * (chosen - jnp.log(totals))
    doc_of = jnp.sum(
        jnp.where(slot_ids[None, :] == seg_share[:, None], doc_index[0][None, :], 0), axis=1
    )
    doc_total = seg_count * lax.axis_size("dp")
    doc_match = (doc_of[:, None] == jnp.arange(doc_total, dtype=jnp.int32)[None, :]).astype(
        jnp.float32
    )
    doc_loglik, doc_counts = in_one(
        (
            jnp.sum(logprob[:, None] * doc_match, axis=0),
            jnp.sum(counted[:, None] * doc_match, axis=0),
        ),
        (("dp", "seq"), ("tensor_0", "tensor_1")),
    )
    token_logprob = collect(logprob, TENSOR, 0)
    return (token_logprob[None, :], doc_loglik, doc_counts)


def solution(mesh):
    split = Mesh(
        mesh.devices.reshape(mesh.shape["dp"], mesh.shape["seq"], 4, 2),
        ("dp", "seq", "tensor_0", "tensor_1"),
    )
    in_specs = (
        P(("dp", "seq"), TENSOR),
        P(("dp", "seq"), TENSOR),
        P(("dp", "seq"), TENSOR),
        P(None, TENSOR),
        P(("dp", "seq"), TENSOR),
        P(TENSOR),
        P(TENSOR),
        P(DP_SEQ_TENSOR, None),
        P("dp", "seq"),
        P("dp", None),
        P("dp", None),
        P(),
    )
    out_specs = (P("dp", "seq"), P(), P())
    return jax.shard_map(local, mesh=split, in_specs=in_specs, out_specs=out_specs, check_vma=False)
```

profile of v0, /device:TPU:1, one launch (start us, length us, event | category | flops | bytes accessed | tf_op | source)
XLA Modules:
  0.0 293.5 jit_solution(2052544937219092689)
XLA Ops:
  7.3 0.9 pad_maximum_fusion
  8.2 23.8 %all_gather.6 = bf16[448,512]{1,0:T(8,128)(2,1)S(1)} all-gather(bf16[56,512]{1,0:T(8,128)(2,1)S(1)} %pad_maximum_fusion), channel_id=1, replica_groups=mesh['dp'=4,'seq'=8,'tensor_0'=4,'tensor_1'=2] {'seq'}, dimensions={0}, use_global_device_ids=true | all-gather | bytes 516096 | tf_op jit(solution)/shard_map/all_gather | solution.py:24
  32.0 0.8 select_reduce_fusion.3
  32.8 1.2 fusion.25
  34.3 19.9 %all_to_all.62 = bf16[8,56,512]{2,1,0:T(8,128)(2,1)S(1)} all-to-all(bf16[8,56,512]{2,1,0:T(8,128)(2,1)S(1)} %broadcast_in_dim.123), channel_id=1, replica_groups=mesh['dp'=4,'seq'=8,'tensor_0'=4,'tensor_1'=2] {'tensor_0','tensor_1'}, dimensions={0} | all-to-all | bytes 917504 | tf_op jit(solution)/shard_map/all_to_all | solution.py:35
  54.3 1.3 fusion.11
  55.7 7.9 %all_to_all.63 = f32[8,1,224]{2,1,0:T(1,128)S(1)} all-to-all(f32[8,1,224]{2,1,0:T(1,128)S(1)} %broadcast_in_dim.124), channel_id=1, replica_groups=mesh['dp'=4,'seq'=8,'tensor_0'=4,'tensor_1'=2] {'tensor_0','tensor_1'}, dimensions={0} | all-to-all | bytes 14336 | tf_op jit(solution)/shard_map/all_to_all | solution.py:35
  63.8 11.8 %all_to_all.64 = bf16[8,56,448]{2,1,0:T(8,128)(2,1)S(1)} all-to-all(bf16[8,56,448]{2,1,0:T(8,128)(2,1)S(1)} %broadcast_in_dim.125), channel_id=1, replica_groups=mesh['dp'=4,'seq'=8,'tensor_0'=4,'tensor_1'=2] {'tensor_0','tensor_1'}, dimensions={0} | all-to-all | bytes 802816 | tf_op jit(solution)/shard_map/all_to_all | solution.py:35
  75.8 1.3 reshape.140
  77.5 117.7 %all-gather.2.cloned.1.call-done = bf16[1792,3584]{1,0:T(8,128)(2,1)} async-done(((bf16[56,3584]{1,0:T(8,128)(2,1)}), bf16[1792,3584]{1,0:T(8,128)(2,1)}) %all-gather.2.cloned.1.call-update) | async-done | bytes 12845072 | tf_op jit(solution)/shard_map/all_gather | solution.py:168
  195.1 12.4 %fusion.1 = (f32[1792]{0:T(1024)S(1)}, f32[1792]{0:T(1024)S(1)}) fusion(s32[1792]{0:T(1024)S(1)} %eq.77, s32[500]{0:T(512)S(1)} %iota_add_fusion, bf16[1792,3584]{1,0:T(8,128)(2,1)} %all-gather.2.cloned.1.call-done, bf16[500,3584]{1,0:T(8,128)(2,1)} %param.19), kind=kOutput, calls=%fused_computation.3 | convolution fusion | flops 6427899904 | bytes 16452560 | tf_op jit(solution)/shard_map/dot_general | solution.py:169
  208.6 5.3 %all-to-all-start.3 = ((f32[8,1,224]{2,1,0:T(1,128)}), f32[8,1,224]{2,1,0:T(1,128)S(1)}, u32[]{:S(2)}, u32[]{:S(2)}) async-start(f32[8,1,224]{2,1,0:T(1,128)} %reshape.153), calls=%async_computation.3 | async-start | bytes 16384 | tf_op jit(solution)/shard_map/all_to_all | solution.py:63
  215.0 3.5 %all-to-all-done.3 = f32[8,1,224]{2,1,0:T(1,128)S(1)} async-done(((f32[8,1,224]{2,1,0:T(1,128)}), f32[8,1,224]{2,1,0:T(1,128)S(1)}, u32[]{:S(2)}, u32[]{:S(2)}) %all-to-all-start.3) | async-done | bytes 7200 | tf_op jit(solution)/shard_map/all_to_all | solution.py:63
  218.5 3.9 %all-to-all-start.5 = ((f32[8,1,224]{2,1,0:T(1,128)}), f32[8,1,224]{2,1,0:T(1,128)S(1)}, u32[]{:S(2)}, u32[]{:S(2)}) async-start(f32[8,1,224]{2,1,0:T(1,128)} %reshape.155), calls=%async_computation.5 | async-start | bytes 16384 | tf_op jit(solution)/shard_map/all_to_all | solution.py:63
  224.4 2.7 all-to-all-done.5
  227.1 5.4 %all-to-all-start.4 = ((f32[32,1,7]{2,1,0:T(1,128)}), f32[32,1,7]{2,1,0:T(1,128)S(1)}, u32[]{:S(2)}, u32[]{:S(2)}) async-start(f32[32,1,7]{2,1,0:T(1,128)} %copy.46), calls=%async_computation.4 | async-start | bytes 32768 | tf_op jit(solution)/shard_map/all_to_all | solution.py:71
  233.9 7.2 %all-to-all-done.4 = f32[32,1,7]{2,1,0:T(1,128)S(1)} async-done(((f32[32,1,7]{2,1,0:T(1,128)}), f32[32,1,7]{2,1,0:T(1,128)S(1)}, u32[]{:S(2)}, u32[]{:S(2)}) %all-to-all-start.4) | async-done | bytes 928 | tf_op jit(solution)/shard_map/all_to_all | solution.py:71
  241.1 3.8 %all-to-all-start.6 = ((f32[32,1,7]{2,1,0:T(1,128)}), f32[32,1,7]{2,1,0:T(1,128)S(1)}, u32[]{:S(2)}, u32[]{:S(2)}) async-start(f32[32,1,7]{2,1,0:T(1,128)} %copy.48), calls=%async_computation.6 | async-start | bytes 32768 | tf_op jit(solution)/shard_map/all_to_all | solution.py:71
  245.1 8.4 %all-to-all-done.6 = f32[32,1,7]{2,1,0:T(1,128)S(1)} async-done(((f32[32,1,7]{2,1,0:T(1,128)}), f32[32,1,7]{2,1,0:T(1,128)S(1)}, u32[]{:S(2)}, u32[]{:S(2)}) %all-to-all-start.6) | async-done | bytes 928 | tf_op jit(solution)/shard_map/all_to_all | solution.py:71
  253.7 10.2 %all_to_all.65 = f32[8,1,64]{2,1,0:T(1,128)S(1)} all-to-all(f32[8,1,64]{2,1,0:T(1,128)S(1)} %broadcast_in_dim.130), channel_id=1, replica_groups=mesh['dp'=4,'seq'=8,'tensor_0'=4,'tensor_1'=2] {'tensor_0','tensor_1'}, dimensions={0} | all-to-all | bytes 4096 | tf_op jit(solution)/shard_map/all_to_all | solution.py:35
  264.5 3.9 %all-to-all-start.7 = ((f32[8,1,7]{2,1,0:T(1,128)}), f32[8,1,7]{2,1,0:T(1,128)S(1)}, u32[]{:S(2)}, u32[]{:S(2)}) async-start(f32[8,1,7]{2,1,0:T(1,128)} %broadcast_in_dim.127), calls=%async_computation.7 | async-start | bytes 8192 | tf_op jit(solution)/shard_map/all_to_all | solution.py:35
  268.4 4.6 %all-to-all-done.7 = f32[8,1,7]{2,1,0:T(1,128)S(1)} async-done(((f32[8,1,7]{2,1,0:T(1,128)}), f32[8,1,7]{2,1,0:T(1,128)S(1)}, u32[]{:S(2)}, u32[]{:S(2)}) %all-to-all-start.7) | async-done | bytes 256 | tf_op jit(solution)/shard_map/all_to_all | solution.py:35
  273.6 3.9 %all-to-all-start.9 = ((f32[32,1,64]{2,1,0:T(1,128)}), f32[32,1,64]{2,1,0:T(1,128)S(1)}, u32[]{:S(2)}, u32[]{:S(2)}) async-start(f32[32,1,64]{2,1,0:T(1,128)} %broadcast_in_dim.131), calls=%async_computation.9 | async-start | bytes 32768 | tf_op jit(solution)/shard_map/all_to_all | solution.py:35
  279.2 6.8 %all-to-all-done.9 = f32[32,1,64]{2,1,0:T(1,128)S(1)} async-done(((f32[32,1,64]{2,1,0:T(1,128)}), f32[32,1,64]{2,1,0:T(1,128)S(1)}, u32[]{:S(2)}, u32[]{:S(2)}) %all-to-all-start.9) | async-done | bytes 8224 | tf_op jit(solution)/shard_map/all_to_all | solution.py:35
  (67 shorter events, 10.9 us)
Async XLA Ops:
  7.2 47.0 %copy-start.1 = (bf16[56,448]{1,0:T(8,128)(2,1)S(1)}, bf16[56,448]{1,0:T(8,128)(2,1)}, u32[]{:S(2)}) copy-start(bf16[56,448]{1,0:T(8,128)(2,1)} %param.16) | copy-start | bytes 150532
  7.2 47.0 %copy-start.2 = (f32[448]{0:T(512)S(1)}, f32[448]{0:T(512)}, u32[]{:S(2)}) copy-start(f32[448]{0:T(512)} %param.17) | copy-start | bytes 5380
  7.2 188.0 %all-gather.2.cloned.1.call-start = ((), (), s32[]{:S(2)}) async-start(), calls=%async_computation.10 | async-start | bytes 13246464 | tf_op jit(solution)/shard_map/all_gather | solution.py:168
  7.2 47.0 %copy-start = (bf16[4096,448]{0,1:T(8,128)(2,1)S(1)}, bf16[4096,448]{0,1:T(8,128)(2,1)}, u32[]{:S(2)}) copy-start(bf16[4096,448]{0,1:T(8,128)(2,1)} %param.15) | copy-start | bytes 11010052
  34.2 29.5 %copy-start.4 = (f32[448]{0:T(512)S(1)}, f32[448]{0:T(512)}, u32[]{:S(2)}) copy-start(f32[448]{0:T(512)} %param.18) | copy-start | bytes 5380
  54.2 22.9 %copy-start.3 = (s32[4,448]{1,0:T(4,128)S(1)}, s32[4,448]{1,0:T(4,128)}, u32[]{:S(2)}) copy-start(s32[4,448]{1,0:T(4,128)} %param.23) | copy-start | bytes 21508
  54.2 23.0 %copy-start.5 = (s32[1,56]{1,0:T(1,128)S(1)}, s32[1,56]{1,0:T(1,128)}, u32[]{:S(2)}) copy-start(s32[1,56]{1,0:T(1,128)} %param.20) | copy-start | bytes 676
  54.3 23.0 %copy-start.6 = (s32[1,8]{1,0:T(1,128)S(1)}, s32[1,8]{1,0:T(1,128)}, u32[]{:S(2)}) copy-start(s32[1,8]{1,0:T(1,128)} %param.21) | copy-start | bytes 100
  77.5 167.4 %copy-start.7 = (s32[1,8]{1,0:T(1,128)S(1)}, s32[1,8]{1,0:T(1,128)}, u32[]{:S(2)}) copy-start(s32[1,8]{1,0:T(1,128)} %param.22) | copy-start | bytes 100
  208.6 9.9 %all-to-all-start.3 = ((f32[8,1,224]{2,1,0:T(1,128)}), f32[8,1,224]{2,1,0:T(1,128)S(1)}, u32[]{:S(2)}, u32[]{:S(2)}) async-start(f32[8,1,224]{2,1,0:T(1,128)} %reshape.153), calls=%async_computation.3 | async-start | bytes 16384 | tf_op jit(solution)/shard_map/all_to_all | solution.py:63
  218.5 8.5 %all-to-all-start.5 = ((f32[8,1,224]{2,1,0:T(1,128)}), f32[8,1,224]{2,1,0:T(1,128)S(1)}, u32[]{:S(2)}, u32[]{:S(2)}) async-start(f32[8,1,224]{2,1,0:T(1,128)} %reshape.155), calls=%async_computation.5 | async-start | bytes 16384 | tf_op jit(solution)/shard_map/all_to_all | solution.py:63
  227.1 14.0 %all-to-all-start.4 = ((f32[32,1,7]{2,1,0:T(1,128)}), f32[32,1,7]{2,1,0:T(1,128)S(1)}, u32[]{:S(2)}, u32[]{:S(2)}) async-start(f32[32,1,7]{2,1,0:T(1,128)} %copy.46), calls=%async_computation.4 | async-start | bytes 32768 | tf_op jit(solution)/shard_map/all_to_all | solution.py:71
  241.1 12.4 %all-to-all-start.6 = ((f32[32,1,7]{2,1,0:T(1,128)}), f32[32,1,7]{2,1,0:T(1,128)S(1)}, u32[]{:S(2)}, u32[]{:S(2)}) async-start(f32[32,1,7]{2,1,0:T(1,128)} %copy.48), calls=%async_computation.6 | async-start | bytes 32768 | tf_op jit(solution)/shard_map/all_to_all | solution.py:71
  264.5 8.5 %all-to-all-start.7 = ((f32[8,1,7]{2,1,0:T(1,128)}), f32[8,1,7]{2,1,0:T(1,128)S(1)}, u32[]{:S(2)}, u32[]{:S(2)}) async-start(f32[8,1,7]{2,1,0:T(1,128)} %broadcast_in_dim.127), calls=%async_computation.7 | async-start | bytes 8192 | tf_op jit(solution)/shard_map/all_to_all | solution.py:35
  273.6 12.5 %all-to-all-start.9 = ((f32[32,1,64]{2,1,0:T(1,128)}), f32[32,1,64]{2,1,0:T(1,128)S(1)}, u32[]{:S(2)}, u32[]{:S(2)}) async-start(f32[32,1,64]{2,1,0:T(1,128)} %broadcast_in_dim.131), calls=%async_computation.9 | async-start | bytes 32768 | tf_op jit(solution)/shard_map/all_to_all | solution.py:35
Sparse Core Ops, SparseCore 0:
  77.2 117.8 all-gather.1
where the time goes:
time: 294 us
  waiting for transfers between devices  151 us (51%)
  blocking collectives  73.6 us (25%)
  starting transfers between devices  26.2 us (9%)
  matrix products  15 us (5%)
  between operations  14.3 us (5%)
  local copies, waits for them, and re-layouts  8.64 us (3%)
  other arithmetic  4.93 us (2%)
    all_gather x1, waiting for transfers between devices, local(): block_in = lax.all_gather(features, ('dp', 'seq'), axis=0, tiled=True)  118 us
    all_to_all x4, blocking collectives, copy_for_each(): lax.all_to_all(jnp.broadcast_to(shard[None], (size, *shard.shape)), axis,...  49.8 us
    all_gather x1, blocking collectives, side_by_side(): lax.all_gather(both, axis, axis=dim, tiled=True)  23.8 us
    all_to_all x2, waiting for transfers between devices, summed_rows(): lax.all_to_all(nearer, far, split_axis=0, concat_axis=0, tiled=True)  15.6 us
    dot_general x1, matrix products, local(): lax.dot_general(vocab_weight, block_in, (((1,), (1,)), ((), ())), preferr...  12.4 us
    all_to_all x2, waiting for transfers between devices, copy_for_each(): lax.all_to_all(jnp.broadcast_to(shard[None], (size, *shard.shape)), axis,...  11.4 us
    all_to_all x2, starting transfers between devices, summed_on_arrival(): blocks = lax.all_to_all(cut_along(shard, dim, size), axis, 0, 0, tiled=True)  9.24 us
    all_to_all x2, starting transfers between devices, summed_rows(): lax.all_to_all(nearer, far, split_axis=0, concat_axis=0, tiled=True)  9.13 us
  transfers between devices with their start and end apart: 7, of which 7 were waited for; matrix products, arithmetic and copies ran while one was open for 2% of the time, Pallas kernels for 0%

commit v1 on v0

--- a/solution.py
+++ b/solution.py
@@ -53,38 +53,61 @@
     return tuple((total[b:e].reshape(a.shape) for a, b, e in zip(arrays, ends, ends[1:])))
 
 
-def cut_along(shard, dim, size):
-    before, after = (shard.shape[:dim], shard.shape[dim + 1 :])
-    return jnp.moveaxis(shard.reshape(*before, size, -1, *after), dim, 0)
-
-
-def summed_on_arrival(shard, axis, dim):
-    size = lax.axis_size(axis)
-    blocks = lax.all_to_all(cut_along(shard, dim, size), axis, 0, 0, tiled=True)
-    return jnp.sum(blocks, axis=0)
-
-
-def summed_rows(shard, axes, dim):
-    far, near = axes
-    blocks = cut_along(shard, dim, lax.axis_size(far))
-    nearer = summed_on_arrival(blocks, near, dim + 1)
-    arrived = lax.all_to_all(nearer, far, split_axis=0, concat_axis=0, tiled=True)
-    return arrived.sum(axis=0)
-
-
-def over_axes(shard, axes):
-    far, near = axes
-    nearer = over_copies(shard, near)
-    return over_copies(nearer, far)
-
-
-def in_one(arrays, axis):
-    flat, at, finished = (jnp.concatenate([a.reshape(-1) for a in arrays]), 0, [])
-    total = over_axes(flat, axis)
-    for a in arrays:
-        finished.append(total[at : at + a.size].reshape(a.shape))
-        at += a.size
-    return tuple(finished)
+def swapped(x):
+    return lax.ppermute(x, "tensor_1", [(0, 1), (1, 0)])
+
+
+def along_x(x, step):
+    size = lax.axis_size("dp")
+    return lax.ppermute(x, "dp", [(i, (i + step) % size) for i in range(size)])
+
+
+def shared_vocabulary(vocab_weight):
+    count = vocab_weight.shape[0]
+    cut = count // 16 * 8 + 8
+    dp_size, seq_size = lax.axis_size("dp"), lax.axis_size("seq")
+    tensor_size = lax.axis_size(TENSOR)
+    dp, seq = lax.axis_index("dp"), lax.axis_index("seq")
+    place, core = lax.axis_index(TENSOR), lax.axis_index("tensor_1")
+    partner = place + 1 - 2 * core
+
+    def first(chip_x, slot):
+        return ((chip_x % dp_size * seq_size + seq) * tensor_size + slot) * count
+
+    from_left = along_x(vocab_weight[:cut], 1)
+    from_right = along_x(vocab_weight[cut:], -1)
+    left, right = dp + dp_size - 1, dp + 1
+    return (
+        (vocab_weight, first(dp, place)),
+        (swapped(vocab_weight), first(dp, partner)),
+        (from_left, first(left, place)),
+        (swapped(from_left), first(left, partner)),
+        (from_right, first(right, place) + cut),
+        (swapped(from_right), first(right, partner) + cut),
+    )
+
+
+def row_features(hidden, on_first):
+    size = lax.axis_size("dp")
+    same, cross = [], []
+    for x in range(size):
+        after, before = (x + 1) % size, (x - 1) % size
+        same += [(2 * x, 2 * before), (2 * x + 1, 2 * after + 1)]
+        cross += [(2 * x, 2 * after + 1), (2 * x + 1, 2 * before)]
+    a = lax.ppermute(hidden, ("dp", "tensor_1"), same)
+    b = lax.ppermute(hidden, ("dp", "tensor_1"), cross)
+    return jnp.concatenate([jnp.where(on_first, a, b), jnp.where(on_first, b, a)], axis=1)
+
+
+def vocabulary_sums(piece, block_in, labels, first_id):
+    logits = lax.dot_general(
+        piece, block_in, (((1,), (1,)), ((), ())), preferred_element_type=jnp.float32
+    )
+    capped = LOGIT_CAP * jnp.tanh(logits / LOGIT_CAP)
+    ids = first_id + jnp.arange(piece.shape[0], dtype=jnp.int32)
+    totals = jnp.sum(jnp.exp(capped), axis=0)
+    chosen = jnp.sum(jnp.where(ids[:, None] == labels[None, :], capped, 0.0), axis=0)
+    return totals, chosen
 
 
 def local(
@@ -114,7 +137,10 @@
     group_size = query_vectors.shape[1] // key_vectors.shape[1]
     query_heads = query_vectors.reshape(tok_rows, local_groups, group_size, HEAD_DIM)
     score_scale = HEAD_DIM ** (-0.5)
-    key_block, value_block = side_by_side((key_vectors, value_vectors), "seq", 0, 1)
+    weight_pieces = shared_vocabulary(vocab_weight)
+    kv_width = key_vectors.shape[1]
+    both = collect(jnp.concatenate((key_vectors, value_vectors), axis=1), "seq", 0)
+    key_block, value_block = both[:, :kv_width], both[:, kv_width:]
     row_count = key_block.shape[0]
     key_heads = key_block.reshape(row_count, local_groups, HEAD_DIM)
     value_heads = value_block.reshape(row_count, local_groups, HEAD_DIM)
@@ -156,54 +182,60 @@
     hidden = (final_gain[None, :] * updated / jnp.sqrt(sq_total / D + EPSILON)[:, None]).astype(
         jnp.bfloat16
     )
-    vocab_count = vocab_weight.shape[0]
-    tensor_size = lax.axis_size(TENSOR)
+    dp_size = lax.axis_size("dp")
     seq_size = lax.axis_size("seq")
-    labels = targets.reshape(-1)
-    flat_index = (
-        lax.axis_index("dp") * seq_size + lax.axis_index("seq")
-    ) * tensor_size + lax.axis_index(TENSOR)
-    vocab_ids = flat_index * vocab_count + jnp.arange(vocab_count, dtype=jnp.int32)
-    features = collect(hidden, TENSOR, 1)
-    block_in = lax.all_gather(features, ("dp", "seq"), axis=0, tiled=True)
-    logits = lax.dot_general(
-        vocab_weight, block_in, (((1,), (1,)), ((), ())), preferred_element_type=jnp.float32
-    )
-    capped = LOGIT_CAP * jnp.tanh(logits / LOGIT_CAP)
-    totals = jnp.sum(jnp.exp(capped), axis=0)
-    chosen = jnp.sum(jnp.where(vocab_ids[:, None] == labels[None, :], capped, 0.0), axis=0)
-    partial_value = jnp.stack([totals, chosen])
-    totals, chosen = (
-        summed_rows(partial_value[0], (("dp", "seq"), ("tensor_0", "tensor_1")), 0),
-        summed_rows(partial_value[1], (("dp", "seq"), ("tensor_0", "tensor_1")), 0),
-    )
-    share_len = totals.shape[0]
-    offset_rows = lax.axis_index(TENSOR) * share_len
-    seg_share = lax.dynamic_slice_in_dim(seg_row, offset_rows, share_len)
-    pos_share = lax.dynamic_slice_in_dim(positions, offset_rows, share_len)
-    next_segment = seg_share + 1
-    doc_end = jnp.sum(
-        jnp.where(slot_ids[None, :] == next_segment[:, None], starts[None, :], 0), axis=1
-    )
-    doc_end = doc_end + jnp.where(next_segment == seg_count, tok_rows * seq_size, 0)
-    counted = (pos_share + 1 < doc_end).astype(jnp.float32)
+    row_len = tok_rows * seq_size
+    on_first = lax.axis_index("tensor_1") == 0
+    taken_row = (lax.axis_index("dp") + jnp.where(on_first, 1, dp_size - 1)) % dp_size
+    features = collect(row_features(hidden, on_first), "tensor_0", 1)
+    block_in = lax.all_gather(features, "seq", axis=0, tiled=True)
+    labels = lax.dynamic_index_in_dim(targets, taken_row, 0, keepdims=False)
+    totals = jnp.zeros((row_len,), jnp.float32)
+    chosen = jnp.zeros((row_len,), jnp.float32)
+    for piece, first_id in weight_pieces:
+        part_total, part_chosen = vocabulary_sums(piece, block_in, labels, first_id)
+        totals, chosen = totals + part_total, chosen + part_chosen
+    tile = (8, 128)
+    spare = jnp.zeros((tile[0] * tile[1] - 2 * row_len,), jnp.float32)
+    sums = over_copies(jnp.concatenate([totals, chosen, spare]).reshape(tile), "tensor_0").ravel()
+    spare = jnp.zeros((tile[0] * tile[1] - 2 * row_len - 2 * seg_count,), jnp.float32)
+    packed = jnp.concatenate(
+        [
+            sums[: 2 * row_len],
+            starts.astype(jnp.float32),
+            doc_index[0].astype(jnp.float32),
+            spare,
+        ]
+    )
+    arrived = copy_for_each(packed.reshape(tile), ("dp", "seq"))
+    arrived = arrived.reshape(dp_size, seq_size, tile[0] * tile[1])
+    own = jnp.sum(arrived[:, :, : 2 * row_len], axis=1)
+    segments = arrived[:, 0, 2 * row_len : 2 * row_len + 2 * seg_count].astype(jnp.int32)
+    other = lax.ppermute(own, "tensor_1", [(0, 1), (1, 0)])
+    below, above = jnp.where(on_first, own, other), jnp.where(on_first, other, own)
+    complete = jnp.roll(below, 1, axis=0) + jnp.roll(above, -1, axis=0)
+    totals, chosen = complete[:, :row_len], complete[:, row_len:]
+    all_starts, all_docs = segments[:, :seg_count], segments[:, seg_count:]
+    places = jnp.arange(row_len, dtype=jnp.int32)
+    ends = jnp.concatenate(
+        [all_starts[:, 1:], jnp.full((dp_size, 1), row_len, jnp.int32)], axis=1
+    )
+    inside = (places[None, None, :] >= all_starts[:, :, None]) & (
+        places[None, None, :] < ends[:, :, None]
+    )
+    last = jnp.sum(jnp.where(inside, ends[:, :, None], 0), axis=1)
+    counted = (places[None, :] + 1 < last).astype(jnp.float32)
     logprob = counted * (chosen - jnp.log(totals))
-    doc_of = jnp.sum(
-        jnp.where(slot_ids[None, :] == seg_share[:, None], doc_index[0][None, :], 0), axis=1
-    )
-    doc_total = seg_count * lax.axis_size("dp")
-    doc_match = (doc_of[:, None] == jnp.arange(doc_total, dtype=jnp.int32)[None, :]).astype(
-        jnp.float32
-    )
-    doc_loglik, doc_counts = in_one(
-        (
-            jnp.sum(logprob[:, None] * doc_match, axis=0),
-            jnp.sum(counted[:, None] * doc_match, axis=0),
-        ),
-        (("dp", "seq"), ("tensor_0", "tensor_1")),
-    )
-    token_logprob = collect(logprob, TENSOR, 0)
-    return (token_logprob[None, :], doc_loglik, doc_counts)
+    seg_loglik = jnp.sum(jnp.where(inside, logprob[:, None, :], 0.0), axis=2)
+    seg_counts = jnp.sum(jnp.where(inside, counted[:, None, :], 0.0), axis=2)
+    doc_total = seg_count * dp_size
+    doc_match = all_docs[None, :, :] == jnp.arange(doc_total, dtype=jnp.int32)[:, None, None]
+    doc_loglik = jnp.sum(jnp.where(doc_match, seg_loglik[None], 0.0), axis=(1, 2))
+    doc_counts = jnp.sum(jnp.where(doc_match, seg_counts[None], 0.0), axis=(1, 2))
+    token_logprob = lax.dynamic_slice(
+        logprob, (lax.axis_index("dp"), lax.axis_index("seq") * tok_rows), (1, tok_rows)
+    )
+    return (token_logprob, doc_loglik, doc_counts)
 
 
 def solution(mesh):

time: 294 us -> 179 us (0.61)
  waiting for transfers between devices: 151 us -> 67.2 us
  blocking collectives: 73.6 us -> 31.1 us
  matrix products: 15 us -> 22.4 us
  starting transfers between devices: 26.2 us -> 32.6 us
    all_gather x1, waiting for transfers between devices: 118 us -> 0.01 us  [local(): block_in = lax.all_gather(features, 'seq', axis=0, tiled=True)]
    ppermute x0 -> x8, waiting for transfers between devices: none -> 38.4 us  [the longest x2 35.5 us: along_x(): return lax.ppermute(x, 'dp', [(i, (i + step) % size) for i in range(size)])]
    all_gather x1 -> x0, blocking collectives: 23.8 us -> none  [side_by_side(): lax.all_gather(both, axis, axis=dim, tiled=True)]
    all_to_all x4 -> x0, waiting for transfers between devices: 21.8 us -> none  [the longest x2 15.6 us: summed_rows(): lax.all_to_all(nearer, far, split_axis=0, concat_axis=0, tiled=True)]
    all_to_all x4 -> x3, blocking collectives: 49.8 us -> 31.1 us  [copy_for_each(): lax.all_to_all(jnp.broadcast_to(shard[None], (size, *shard.shape)), axis,...]
    all_to_all x4 -> x0, starting transfers between devices: 18.4 us -> none  [the longest x2 9.24 us: summed_on_arrival(): blocks = lax.all_to_all(cut_along(shard, dim, size), axis, 0, 0, tiled=True)]
    all_to_all x2 -> x3, waiting for transfers between devices: 11.4 us -> 28.8 us  [copy_for_each(): lax.all_to_all(jnp.broadcast_to(shard[None], (size, *shard.shape)), axis,...]
    ppermute x0 -> x8, starting transfers between devices: none -> 15.4 us  [the longest x3 4.73 us: swapped(): return lax.ppermute(x, 'tensor_1', [(0, 1), (1, 0)])]
  transfers between devices with their start and end apart: 7 -> 12, of which waited for: 7 -> 8; matrix products, arithmetic and copies ran while one was open for 2% -> 12% of each run, Pallas kernels for 0% -> 0%
where the time goes in v1:
time: 179 us; the launch traced here: 178 us
  waiting for transfers between devices  67.2 us (38%)
  starting transfers between devices  32.6 us (18%)
  blocking collectives  31.1 us (17%)
  matrix products  22.4 us (13%)
  between operations  14.4 us (8%)
  local copies, waits for them, and re-layouts  7.09 us (4%)
  other arithmetic  3.29 us (2%)
    ppermute x2, waiting for transfers between devices, along_x(): return lax.ppermute(x, 'dp', [(i, (i + step) % size) for i in range(size)])  35.5 us
    all_to_all x3, blocking collectives, copy_for_each(): lax.all_to_all(jnp.broadcast_to(shard[None], (size, *shard.shape)), axis,...  31.1 us
    all_to_all x3, waiting for transfers between devices, copy_for_each(): lax.all_to_all(jnp.broadcast_to(shard[None], (size, *shard.shape)), axis,...  28.8 us
    dot_general x6, matrix products, vocabulary_sums(): lax.dot_general(piece, block_in, (((1,), (1,)), ((), ())), preferred_elem...  19.6 us
    all_to_all x3, starting transfers between devices, copy_for_each(): lax.all_to_all(jnp.broadcast_to(shard[None], (size, *shard.shape)), axis,...  17.2 us
    ppermute x3, starting transfers between devices, swapped(): return lax.ppermute(x, 'tensor_1', [(0, 1), (1, 0)])  4.73 us
    ppermute x2, starting transfers between devices, along_x(): return lax.ppermute(x, 'dp', [(i, (i + step) % size) for i in range(size)])  4.02 us
  transfers between devices with their start and end apart: 12, of which 8 were waited for; matrix products, arithmetic and copies ran while one was open for 12% of the time, Pallas kernels for 0%

profile of v1, /device:TPU:1, one launch (start us, length us, event | category | flops | bytes accessed | tf_op | source)
XLA Modules:
  0.0 178.1 jit_solution(13312510431520741141)
XLA Ops:
  8.8 9.0 %all-to-all-start = ((bf16[8,56,512]{2,1,0:T(8,128)(2,1)}), bf16[8,56,512]{2,1,0:T(8,128)(2,1)S(1)}, u32[]{:S(2)}, u32[]{:S(2)}) async-start(bf16[8,56,512]{2,1,0:T(8,128)(2,1)} %broadcast_in_dim.166), calls=%async_computation | async-start | bytes 917504 | tf_op jit(solution)/shard_map/all_to_all | solution.py:35
  18.7 15.5 %all-to-all-done = bf16[8,56,512]{2,1,0:T(8,128)(2,1)S(1)} async-done(((bf16[8,56,512]{2,1,0:T(8,128)(2,1)}), bf16[8,56,512]{2,1,0:T(8,128)(2,1)S(1)}, u32[]{:S(2)}, u32[]{:S(2)}) %all-to-all-start) | async-done | bytes 458784 | tf_op jit(solution)/shard_map/all_to_all | solution.py:35
  35.9 13.6 %all_to_all.31 = bf16[8,56,512]{2,1,0:T(8,128)(2,1)S(1)} all-to-all(bf16[8,56,512]{2,1,0:T(8,128)(2,1)S(1)} %broadcast_in_dim.172), channel_id=1, replica_groups=mesh['dp'=4,'seq'=8,'tensor_0'=4,'tensor_1'=2] {'tensor_0','tensor_1'}, dimensions={0} | all-to-all | bytes 917504 | tf_op jit(solution)/shard_map/all_to_all | solution.py:35
  51.0 7.9 %all_to_all.32 = f32[8,1,224]{2,1,0:T(1,128)S(1)} all-to-all(f32[8,1,224]{2,1,0:T(1,128)S(1)} %broadcast_in_dim.173), channel_id=1, replica_groups=mesh['dp'=4,'seq'=8,'tensor_0'=4,'tensor_1'=2] {'tensor_0','tensor_1'}, dimensions={0} | all-to-all | bytes 14336 | tf_op jit(solution)/shard_map/all_to_all | solution.py:35
  60.4 2.7 %collective-permute-start.1 = (bf16[56,448]{1,0:T(8,128)(2,1)S(1)}, bf16[56,448]{1,0:T(8,128)(2,1)S(1)}, u32[]{:S(2)}, u32[]{:S(2)}) collective-permute-start(bf16[56,448]{1,0:T(8,128)(2,1)S(1)} %fusion.30), channel_id=1, source_target_pairs={{0,65},{1,192},{64,129},{65,0},{128,193},{129,64},{192,1},{193,128... | collective-permute-start | bytes 150536 | tf_op jit(solution)/shard_map/ppermute | solution.py:98
  63.4 1.8 %collective-permute-done.1 = bf16[56,448]{1,0:T(8,128)(2,1)S(1)} collective-permute-done((bf16[56,448]{1,0:T(8,128)(2,1)S(1)}, bf16[56,448]{1,0:T(8,128)(2,1)S(1)}, u32[]{:S(2)}, u32[]{:S(2)}) %collective-permute-start.1) | collective-permute-done | bytes 50208 | tf_op jit(solution)/shard_map/ppermute | solution.py:98
  65.3 9.5 %all_to_all.33 = bf16[4,56,896]{2,1,0:T(8,128)(2,1)S(1)} all-to-all(bf16[4,56,896]{2,1,0:T(8,128)(2,1)S(1)} %broadcast_in_dim.174), channel_id=1, replica_groups=mesh['dp'=4,'seq'=8,'tensor_0'=4,'tensor_1'=2] {'tensor_0'}, dimensions={0} | all-to-all | bytes 802816 | tf_op jit(solution)/shard_map/all_to_all | solution.py:35
  75.7 1.6 slice.74
  77.4 1.9 %collective-permute-start.3 = (bf16[256,3584]{1,0:T(8,128)(2,1)S(1)}, bf16[256,3584]{1,0:T(8,128)(2,1)}, u32[]{:S(2)}, u32[]{:S(2)}) collective-permute-start(bf16[256,3584]{1,0:T(8,128)(2,1)S(1)} %slice.74), channel_id=1, source_target_pairs={{0,64},{64,128},{128,192},{192,0},{1,65},{65,129},{129,193},{193,1... | collective-permute-start | bytes 5505032 | tf_op jit(solution)/shard_map/ppermute | solution.py:62
  80.3 1.6 slice.75
  81.9 2.1 %collective-permute-start.5 = (bf16[244,3584]{1,0:T(8,128)(2,1)S(1)}, bf16[244,3584]{1,0:T(8,128)(2,1)}, u32[]{:S(2)}, u32[]{:S(2)}) collective-permute-start(bf16[244,3584]{1,0:T(8,128)(2,1)S(1)} %slice.75), channel_id=1, source_target_pairs={{0,192},{64,0},{128,64},{192,128},{1,193},{65,1},{129,65},{193,129... | collective-permute-start | bytes 5246984 | tf_op jit(solution)/shard_map/ppermute | solution.py:62
  84.0 34.3 %collective-permute-done.3 = bf16[256,3584]{1,0:T(8,128)(2,1)} collective-permute-done((bf16[256,3584]{1,0:T(8,128)(2,1)S(1)}, bf16[256,3584]{1,0:T(8,128)(2,1)}, u32[]{:S(2)}, u32[]{:S(2)}) %collective-permute-start.3) | collective-permute-done | bytes 1835040 | tf_op jit(solution)/shard_map/ppermute | solution.py:62
  118.3 2.9 %collective-permute-start.4 = (bf16[256,3584]{1,0:T(8,128)(2,1)}, bf16[256,3584]{1,0:T(8,128)(2,1)}, u32[]{:S(2)}, u32[]{:S(2)}) collective-permute-start(bf16[256,3584]{1,0:T(8,128)(2,1)} %collective-permute-done.3), channel_id=1, source_target_pairs={{0,1},{1,0},{2,3},{3,2},{4,5},{5,4},{6,7},{7,6},{8,9},{9,8},{10,11... | collective-permute-start | bytes 5505032 | tf_op jit(solution)/shard_map/ppermute | solution.py:57
  123.3 3.6 %fusion.17 = f32[256,448]{0,1:T(8,128)S(1)} fusion(bf16[448,3584]{1,0:T(8,128)(2,1)} %all-gather.2.cloned.1.call-done, bf16[256,3584]{1,0:T(8,128)(2,1)} %collective-permute-done.3), kind=kOutput, calls=%fused_computation.23 | convolution fusion | flops 822312960 | bytes 5505024 | tf_op jit(solution)/shard_map/dot_general | solution.py:103
  127.0 2.5 %fusion.11 = f32[244,448]{0,1:T(8,128)S(1)} fusion(bf16[448,3584]{1,0:T(8,128)(2,1)S(1)} %copy-done.7, bf16[244,3584]{1,0:T(8,128)(2,1)} %collective-permute-done.5), kind=kOutput, calls=%fused_computation.15 | convolution fusion | flops 783767040 | bytes 5397504 | tf_op jit(solution)/shard_map/dot_general | solution.py:103
  129.5 2.7 %exponential_reduce_fusion.5 = (f32[448]{0:T(512)S(1)}, f32[448]{0:T(512)S(1)}, f32[448]{0:T(512)S(1)}, f32[448]{0:T(512)S(1)}) fusion(f32[256,448]{0,1:T(8,128)S(1)} %fusion.17, s32[448]{0:T(512)S(1)} %bitcast.95, s32[256]{0:T(256)S(1)} %iota_add_fusion.6, s32[256]{0:T(256)S(1)} %iota_add_fusion.5, bf16[448,3584]{1,0:T(8,128)(2,1)S(1)} %copy-done.7, ...), kind=kOutput, calls=%fused_computation.45 | convolution fusion | flops 823228672 | bytes 5516032 | tf_op jit(solution)/shard_map/dot_general | solution.py:103
  132.2 3.9 %fusion.5 = f32[500,448]{0,1:T(8,128)S(1)} fusion(bf16[448,3584]{1,0:T(8,128)(2,1)S(1)} %copy-done.7, bf16[500,3584]{1,0:T(8,128)(2,1)} %param.19), kind=kOutput, calls=%fused_computation.7 | convolution fusion | flops 1606080000 | bytes 7691264 | tf_op jit(solution)/shard_map/dot_general | solution.py:103
  136.1 4.2 %exponential_reduce_fusion = (f32[448]{0:T(512)S(1)}, f32[448]{0:T(512)S(1)}, f32[448]{0:T(512)S(1)}, f32[448]{0:T(512)S(1)}) fusion(s32[448]{0:T(512)S(1)} %bitcast.96, s32[500]{0:T(512)S(1)} %iota_add_fusion, f32[500,448]{0,1:T(8,128)S(1)} %fusion.5, s32[500]{0:T(512)S(1)} %iota_add_fusion.1, bf16[448,3584]{1,0:T(8,128)(2,1)S(1)} %copy-done.7, ...), kind=kOutput, calls=%fused_computation.36 | convolution fusion | flops 1607869952 | bytes 7704224 | tf_op jit(solution)/shard_map/dot_general | solution.py:103
  140.4 2.7 %exponential_reduce_fusion.3 = (f32[448]{0:T(512)S(1)}, f32[448]{0:T(512)S(1)}, f32[448]{0:T(512)S(1)}, f32[448]{0:T(512)S(1)}) fusion(f32[244,448]{0,1:T(8,128)S(1)} %fusion.11, s32[448]{0:T(512)S(1)} %bitcast.97, s32[244]{0:T(256)S(1)} %iota_add_fusion.4, s32[244]{0:T(256)S(1)} %iota_add_fusion.3, bf16[448,3584]{1,0:T(8,128)(2,1)S(1)} %copy-done.7, ...), kind=kOutput, calls=%fused_computation.43 | convolution fusion | flops 784639744 | bytes 5408416 | tf_op jit(solution)/shard_map/dot_general | solution.py:103
  143.7 3.2 %all-to-all-start.4 = ((f32[4,8,128]{2,1,0:T(8,128)}), f32[4,8,128]{2,1,0:T(8,128)S(1)}, u32[]{:S(2)}, u32[]{:S(2)}) async-start(f32[4,8,128]{2,1,0:T(8,128)} %broadcast_in_dim.180), calls=%async_computation.4 | async-start | bytes 32768 | tf_op jit(solution)/shard_map/all_to_all | solution.py:35
  147.0 4.1 %all-to-all-done.4 = f32[4,8,128]{2,1,0:T(8,128)S(1)} async-done(((f32[4,8,128]{2,1,0:T(8,128)}), f32[4,8,128]{2,1,0:T(8,128)S(1)}, u32[]{:S(2)}, u32[]{:S(2)}) %all-to-all-start.4) | async-done | bytes 16416 | tf_op jit(solution)/shard_map/all_to_all | solution.py:35
  151.9 4.9 %all-to-all-start.5 = ((f32[32,8,128]{2,1,0:T(8,128)}), f32[32,8,128]{2,1,0:T(8,128)S(1)}, u32[]{:S(2)}, u32[]{:S(2)}) async-start(f32[32,8,128]{2,1,0:T(8,128)} %broadcast_in_dim.183), calls=%async_computation.5 | async-start | bytes 262144 | tf_op jit(solution)/shard_map/all_to_all | solution.py:35
  156.8 9.1 %all-to-all-done.5 = f32[32,8,128]{2,1,0:T(8,128)S(1)} async-done(((f32[32,8,128]{2,1,0:T(8,128)}), f32[32,8,128]{2,1,0:T(8,128)S(1)}, u32[]{:S(2)}, u32[]{:S(2)}) %all-to-all-start.5) | async-done | bytes 131104 | tf_op jit(solution)/shard_map/all_to_all | solution.py:35
  166.2 2.7 %collective-permute-start.7 = (f32[4,896]{1,0:T(4,128)S(1)}, f32[4,896]{1,0:T(4,128)S(1)}, u32[]{:S(2)}, u32[]{:S(2)}) collective-permute-start(f32[4,896]{1,0:T(4,128)S(1)} %slice_reduce_fusion), channel_id=1, source_target_pairs={{0,1},{1,0},{2,3},{3,2},{4,5},{5,4},{6,7},{7,6},{8,9},{9,8},{10,11... | collective-permute-start | bytes 43016 | tf_op jit(solution)/shard_map/ppermute | solution.py:214
  (84 shorter events, 15.5 us)
Async XLA Ops:
  7.2 114.1 %copy-start = (s32[4,448]{1,0:T(4,128)S(1)}, s32[4,448]{1,0:T(4,128)}, u32[]{:S(2)}) copy-start(s32[4,448]{1,0:T(4,128)} %param.23) | copy-start | bytes 21508
  7.2 42.4 %copy-start.2 = (bf16[56,448]{1,0:T(8,128)(2,1)S(1)}, bf16[56,448]{1,0:T(8,128)(2,1)}, u32[]{:S(2)}) copy-start(bf16[56,448]{1,0:T(8,128)(2,1)} %param.16) | copy-start | bytes 150532
  7.2 42.4 %copy-start.3 = (f32[448]{0:T(512)S(1)}, f32[448]{0:T(512)}, u32[]{:S(2)}) copy-start(f32[448]{0:T(512)} %param.17) | copy-start | bytes 5380
  8.8 25.5 %all-to-all-start = ((bf16[8,56,512]{2,1,0:T(8,128)(2,1)}), bf16[8,56,512]{2,1,0:T(8,128)(2,1)S(1)}, u32[]{:S(2)}, u32[]{:S(2)}) async-start(bf16[8,56,512]{2,1,0:T(8,128)(2,1)} %broadcast_in_dim.166), calls=%async_computation | async-start | bytes 917504 | tf_op jit(solution)/shard_map/all_to_all | solution.py:35
  17.8 105.5 %all-gather.2.cloned.1.call-start = ((), (), s32[]{:S(2)}) async-start(), calls=%async_computation.6 | async-start | bytes 3612672 | tf_op jit(solution)/shard_map/all_gather | solution.py:191
  34.3 15.3 %copy-start.1 = (bf16[4096,448]{0,1:T(8,128)(2,1)S(1)}, bf16[4096,448]{0,1:T(8,128)(2,1)}, u32[]{:S(2)}) copy-start(bf16[4096,448]{0,1:T(8,128)(2,1)} %param.15) | copy-start | bytes 11010052
  35.9 23.1 %copy-start.4 = (f32[448]{0:T(512)S(1)}, f32[448]{0:T(512)}, u32[]{:S(2)}) copy-start(f32[448]{0:T(512)} %param.18) | copy-start | bytes 5380
  59.1 4.3 %collective-permute-start = (bf16[56,448]{1,0:T(8,128)(2,1)S(1)}, bf16[56,448]{1,0:T(8,128)(2,1)S(1)}, u32[]{:S(2)}, u32[]{:S(2)}) collective-permute-start(bf16[56,448]{1,0:T(8,128)(2,1)S(1)} %fusion.30), channel_id=1, source_target_pairs={{0,192},{1,65},{64,0},{65,129},{128,64},{129,193},{192,128},{193,1... | collective-permute-start | bytes 150536 | tf_op jit(solution)/shard_map/ppermute | solution.py:97
  60.4 4.8 %collective-permute-start.1 = (bf16[56,448]{1,0:T(8,128)(2,1)S(1)}, bf16[56,448]{1,0:T(8,128)(2,1)S(1)}, u32[]{:S(2)}, u32[]{:S(2)}) collective-permute-start(bf16[56,448]{1,0:T(8,128)(2,1)S(1)} %fusion.30), channel_id=1, source_target_pairs={{0,65},{1,192},{64,129},{65,0},{128,193},{129,64},{192,1},{193,128... | collective-permute-start | bytes 150536 | tf_op jit(solution)/shard_map/ppermute | solution.py:98
  77.4 40.9 %collective-permute-start.3 = (bf16[256,3584]{1,0:T(8,128)(2,1)S(1)}, bf16[256,3584]{1,0:T(8,128)(2,1)}, u32[]{:S(2)}, u32[]{:S(2)}) collective-permute-start(bf16[256,3584]{1,0:T(8,128)(2,1)S(1)} %slice.74), channel_id=1, source_target_pairs={{0,64},{64,128},{128,192},{192,0},{1,65},{65,129},{129,193},{193,1... | collective-permute-start | bytes 5505032 | tf_op jit(solution)/shard_map/ppermute | solution.py:62
  79.3 56.8 %collective-permute-start.2 = (bf16[500,3584]{1,0:T(8,128)(2,1)}, bf16[500,3584]{1,0:T(8,128)(2,1)}, u32[]{:S(2)}, u32[]{:S(2)}) collective-permute-start(bf16[500,3584]{1,0:T(8,128)(2,1)} %param.19), channel_id=1, source_target_pairs={{0,1},{1,0},{2,3},{3,2},{4,5},{5,4},{6,7},{7,6},{8,9},{9,8},{10,11... | collective-permute-start | bytes 10752008 | tf_op jit(solution)/shard_map/ppermute | solution.py:57
  81.9 40.6 %collective-permute-start.5 = (bf16[244,3584]{1,0:T(8,128)(2,1)S(1)}, bf16[244,3584]{1,0:T(8,128)(2,1)}, u32[]{:S(2)}, u32[]{:S(2)}) collective-permute-start(bf16[244,3584]{1,0:T(8,128)(2,1)S(1)} %slice.75), channel_id=1, source_target_pairs={{0,192},{64,0},{128,64},{192,128},{1,193},{65,1},{129,65},{193,129... | collective-permute-start | bytes 5246984 | tf_op jit(solution)/shard_map/ppermute | solution.py:62
  118.3 11.2 %collective-permute-start.4 = (bf16[256,3584]{1,0:T(8,128)(2,1)}, bf16[256,3584]{1,0:T(8,128)(2,1)}, u32[]{:S(2)}, u32[]{:S(2)}) collective-permute-start(bf16[256,3584]{1,0:T(8,128)(2,1)} %collective-permute-done.3), channel_id=1, source_target_pairs={{0,1},{1,0},{2,3},{3,2},{4,5},{5,4},{6,7},{7,6},{8,9},{9,8},{10,11... | collective-permute-start | bytes 5505032 | tf_op jit(solution)/shard_map/ppermute | solution.py:57
  122.5 17.8 %collective-permute-start.6 = (bf16[244,3584]{1,0:T(8,128)(2,1)}, bf16[244,3584]{1,0:T(8,128)(2,1)}, u32[]{:S(2)}, u32[]{:S(2)}) collective-permute-start(bf16[244,3584]{1,0:T(8,128)(2,1)} %collective-permute-done.5), channel_id=1, source_target_pairs={{0,1},{1,0},{2,3},{3,2},{4,5},{5,4},{6,7},{7,6},{8,9},{9,8},{10,11... | collective-permute-start | bytes 5246984 | tf_op jit(solution)/shard_map/ppermute | solution.py:57
  123.3 3.7 %copy-start.7 = (bf16[448,3584]{1,0:T(8,128)(2,1)S(1)}, bf16[448,3584]{1,0:T(8,128)(2,1)}, u32[]{:S(2)}) copy-start(bf16[448,3584]{1,0:T(8,128)(2,1)} %all-gather.2.cloned.1.call-done) | copy-start | bytes 9633796
  140.3 6.7 %copy-start.5 = (s32[1,8]{1,0:T(1,128)S(1)}, s32[1,8]{1,0:T(1,128)}, u32[]{:S(2)}) copy-start(s32[1,8]{1,0:T(1,128)} %param.22) | copy-start | bytes 100
  140.3 6.7 %copy-start.6 = (s32[1,8]{1,0:T(1,128)S(1)}, s32[1,8]{1,0:T(1,128)}, u32[]{:S(2)}) copy-start(s32[1,8]{1,0:T(1,128)} %param.21) | copy-start | bytes 100
  143.7 7.4 %all-to-all-start.4 = ((f32[4,8,128]{2,1,0:T(8,128)}), f32[4,8,128]{2,1,0:T(8,128)S(1)}, u32[]{:S(2)}, u32[]{:S(2)}) async-start(f32[4,8,128]{2,1,0:T(8,128)} %broadcast_in_dim.180), calls=%async_computation.4 | async-start | bytes 32768 | tf_op jit(solution)/shard_map/all_to_all | solution.py:35
  151.9 14.1 %all-to-all-start.5 = ((f32[32,8,128]{2,1,0:T(8,128)}), f32[32,8,128]{2,1,0:T(8,128)S(1)}, u32[]{:S(2)}, u32[]{:S(2)}) async-start(f32[32,8,128]{2,1,0:T(8,128)} %broadcast_in_dim.183), calls=%async_computation.5 | async-start | bytes 262144 | tf_op jit(solution)/shard_map/all_to_all | solution.py:35
  166.2 3.5 %collective-permute-start.7 = (f32[4,896]{1,0:T(4,128)S(1)}, f32[4,896]{1,0:T(4,128)S(1)}, u32[]{:S(2)}, u32[]{:S(2)}) collective-permute-start(f32[4,896]{1,0:T(4,128)S(1)} %slice_reduce_fusion), channel_id=1, source_target_pairs={{0,1},{1,0},{2,3},{3,2},{4,5},{5,4},{6,7},{7,6},{8,9},{9,8},{10,11... | collective-permute-start | bytes 43016 | tf_op jit(solution)/shard_map/ppermute | solution.py:214
Sparse Core Ops, SparseCore 0:
  75.9 39.9 all-gather.1
